TPU v7x, 32 devices: a whole 2x2x4 slice. The times are simulated.
32 devices in a mesh: occ: 4 (over x, core), vir: 8 (over z, y).
Axes of the slice: x: 2, y: 2, z: 4, core: 2. Of those that a mesh axis runs over, the one named last changes fastest.
Arguments:
- amps: bfloat16 [4096, 3072], P('occ', 'vir'), may hold values from -6 to 6
- ints: bfloat16 [3072, 4096], P(None, 'vir'), may hold values from -0.109375 to 0.109375
- amp_mask: int32 [128, 6], P('occ'), may hold values 0 or 1
- keep_mask: int32 [128, 8], P('occ', 'vir'), may hold values 0 or 1
- owners: int32 [128, 1], P('occ'), may hold values from 0 to 3; in each aligned block of 32 rows (0 to 31, 32 to 63, ...) at most 16 rows name the same one
- occ_energy: bfloat16 [4096], P('occ'), may hold values from -2 to -0.5
- vir_energy: float32 [4096], P('vir'), may hold values from 0.5 to 3
- mix: bfloat16 [4, 32, 32], P('occ'), may hold values from -4 to 4
Outputs:
- owned: bfloat16 [256, 32, 4096], P('occ', None, 'vir')
Inputs may be any that keep to these rules, and one draw needn't show every extreme that they name: `owners`: in the row tiles of one index of occ no owner appears more than 16 times; in every draw some owner appears exactly 16 times in some device's tiles.
All inputs are finite; a program needn't handle non-finite values. No bound on the sum of `amp_mask` or of `keep_mask` on one device may be relied on, other than what follows from the above.
Results may differ from a plain program's by a relative error of at most 0.0049.
Values may be sent and summed in bfloat16 or wider, within the bound.
A program may use at most 64 MiB of HBM per device.

v0:
```python
import jax
import jax.numpy as jnp
from jax import lax
from jax.sharding import PartitionSpec as P


def shards(amps, ints, amp_mask, keep_mask, owners, occ_energy, vir_energy, mix):
    tiles_dev, k_tiles = amp_mask.shape
    row_count, k_width = amps.shape
    tile_rows = row_count // tiles_dev
    col_count = ints.shape[1]
    owner_count = lax.axis_size("occ")
    capacity = max(2, 2 * tiles_dev // owner_count)
    slot_count = owner_count * capacity
    k_first = lax.axis_index("vir") * k_width
    column_tile = (k_first + jnp.arange(k_width, dtype=jnp.int32)) // (ints.shape[0] // k_tiles)
    select = (column_tile[None, :] == jnp.arange(k_tiles, dtype=jnp.int32)[:, None]).astype(
        jnp.float32
    )
    col_mask = jnp.dot(amp_mask.astype(jnp.float32), select).astype(jnp.bfloat16)
    masked = amps.reshape(tiles_dev, tile_rows, k_width) * col_mask[:, None, :]
    destination = owners[:, 0]
    same_owner = destination[:, None] == destination[None, :]
    earlier = jnp.arange(tiles_dev)[:, None] > jnp.arange(tiles_dev)[None, :]
    position = jnp.sum((same_owner & earlier).astype(jnp.int32), axis=1)
    slot_index = destination * capacity + position
    routing = (slot_index[None, :] == jnp.arange(slot_count, dtype=jnp.int32)[:, None]).astype(
        jnp.bfloat16
    )
    send_energy = jnp.dot(
        routing, occ_energy.reshape(tiles_dev, tile_rows), preferred_element_type=jnp.float32
    ).astype(jnp.bfloat16)
    keep_flag = keep_mask.astype(jnp.bfloat16)
    weight = mix[0]
    ladder = jnp.dot(
        lax.all_gather(masked.reshape(row_count, k_width), "vir", axis=1, tiled=True),
        ints,
        preferred_element_type=jnp.float32,
    )
    kept_tiles = ladder.astype(jnp.bfloat16).reshape(tiles_dev, tile_rows * col_count) * keep_flag
    send_tiles = jnp.dot(routing, kept_tiles, preferred_element_type=jnp.float32).astype(
        jnp.bfloat16
    )
    tiles_in = lax.all_to_all(
        send_tiles.reshape(owner_count, capacity, tile_rows, col_count),
        "occ",
        split_axis=0,
        concat_axis=0,
        tiled=True,
    )
    energy_in = lax.all_to_all(
        send_energy.reshape(owner_count, capacity, tile_rows),
        "occ",
        split_axis=0,
        concat_axis=0,
        tiled=True,
    )
    mixed_rows = jnp.einsum("ij,oajc->oaic", weight, tiles_in, preferred_element_type=jnp.float32)
    denominator = vir_energy - energy_in.astype(jnp.float32)[..., None]
    owned = (mixed_rows / denominator).astype(jnp.bfloat16)
    owned = owned.reshape(slot_count, tile_rows, col_count)
    return owned


def solution(mesh):
    in_specs = (
        P("occ", "vir"),
        P(None, "vir"),
        P("occ", None),
        P("occ", "vir"),
        P("occ", None),
        P("occ"),
        P("vir"),
        P("occ", None, None),
    )
    out_specs = P("occ", None, "vir")
    return jax.shard_map(shards, mesh=mesh, in_specs=in_specs, out_specs=out_specs, check_vma=False)
```

profile of v0, /device:TPU:1, one launch (start us, length us, event | category | flops | bytes accessed | tf_op | source)
XLA Modules:
  0.0 165.5 jit_solution(3079758830397901695)
XLA Ops:
  6.5 0.0 copy-start
  6.5 0.0 all-gather.2.cloned.1.call-start
  6.6 1.0 fusion.1
  7.6 2.1 %bitcast_multiply_fusion = bf16[1024,384]{1,0:T(8,128)(2,1)} fusion(bf16[1024,384]{1,0:T(8,128)(2,1)} %param.8, bf16[32,384]{1,0:T(8,128)(2,1)S(1)} %fusion.1), kind=kLoop, calls=%fused_computation.8 | loop fusion | flops 393216 | bytes 1597440 | tf_op jit(solution)/shard_map/mul | solution.py:21
  9.7 0.0 all-gather.2.cloned.1.call-update
  9.7 0.8 reshape.51
  10.5 0.9 convert_reduce_fusion
  11.4 0.7 multiply_add_fusion
  12.1 0.2 convolution_convert_fusion.3
  12.2 0.1 copy.11
  12.3 0.7 reshape.55
  13.0 4.3 %all-to-all-start.1 = ((bf16[4,2,256]{2,1,0:T(2,128)(2,1)}), bf16[4,2,256]{2,1,0:T(2,128)(2,1)S(1)}, u32[]{:S(2)}, u32[]{:S(2)}) async-start(bf16[4,2,256]{2,1,0:T(2,128)(2,1)} %reshape.55), calls=%async_computation.1 | async-start | bytes 8192 | tf_op jit(solution)/shard_map/all_to_all | solution.py:51
  17.3 0.7 convert_bitcast_fusion
  17.9 92.7 %all-gather.2.cloned.1.call-done = bf16[1024,3072]{1,0:T(8,128)(2,1)} async-done(((bf16[1024,384]{1,0:T(8,128)(2,1)}), bf16[1024,3072]{1,0:T(8,128)(2,1)}) %all-gather.2.cloned.1.call-update) | async-done | bytes 6291472 | tf_op jit(solution)/shard_map/all_gather | solution.py:36
  110.7 0.0 copy-done
  110.7 7.2 %convolution_convert_fusion.1 = bf16[1024,512]{1,0:T(8,128)(2,1)} fusion(bf16[1024,3072]{1,0:T(8,128)(2,1)} %all-gather.2.cloned.1.call-done, bf16[3072,512]{1,0:T(8,128)(2,1)S(1)} %copy-done), kind=kOutput, calls=%fused_computation.3 | convolution fusion | flops 3221749760 | bytes 10485760 | tf_op jit(solution)/shard_map/dot_general | solution.py:35
  117.8 2.3 %reshape.49 = bf16[32,16384]{1,0:T(8,128)(2,1)} reshape(bf16[1024,512]{1,0:T(8,128)(2,1)} %convolution_convert_fusion.1) | data formatting | bytes 2097152 | tf_op jit(solution)/shard_map/reshape | solution.py:40
  120.2 2.0 %convolution_convert_fusion = bf16[64,16384]{1,0:T(8,128)(2,1)S(1)} fusion(bf16[32,16384]{1,0:T(8,128)(2,1)} %reshape.49, bf16[32]{0:T(256)(128)(2,1)S(1)} %convert_bitcast_fusion, s32[32]{0:T(128)S(1)} %multiply_add_fusion), kind=kOutput, calls=%fused_computation | convolution fusion | flops 68683776 | bytes 3145920 | tf_op jit(solution)/shard_map/dot_general | solution.py:41
  122.1 2.1 %copy.13 = bf16[8,8,32,512]{3,2,1,0:T(8,128)(2,1)} copy(bf16[8,8,32,512]{3,1,2,0:T(8,128)(2,1)S(1)} %bitcast.29) | data formatting | bytes 4194304
  124.2 0.0 copy-start.1
  124.2 0.0 copy-start.2
  124.2 0.0 all-to-all-done.1
  124.2 6.0 %all-to-all-start = ((bf16[4,16,32,512]{3,2,1,0:T(8,128)(2,1)}), bf16[4,16,32,512]{3,2,1,0:T(8,128)(2,1)}, u32[]{:S(2)}, u32[]{:S(2)}) async-start(bf16[4,16,32,512]{3,2,1,0:T(8,128)(2,1)} %bitcast.28), calls=%async_computation | async-start | bytes 4194304 | tf_op jit(solution)/shard_map/all_to_all | solution.py:44
  130.2 0.1 reshape.56
  130.3 24.7 %all-to-all-done = bf16[4,16,32,512]{3,2,1,0:T(8,128)(2,1)} async-done(((bf16[4,16,32,512]{3,2,1,0:T(8,128)(2,1)}), bf16[4,16,32,512]{3,2,1,0:T(8,128)(2,1)}, u32[]{:S(2)}, u32[]{:S(2)}) %all-to-all-start) | async-done | bytes 2097184 | tf_op jit(solution)/shard_map/all_to_all | solution.py:44
  155.0 0.0 copy-done.1
  155.0 0.0 copy-done.2
  155.0 3.7 %fusion = bf16[4,16,32,512]{3,2,1,0:T(8,128)(2,1)} fusion(bf16[4,16,32,512]{3,2,1,0:T(8,128)(2,1)} %all-to-all-done, f32[4,16,32]{2,1,0:T(8,128)S(1)} %convert_element_type.40, f32[512]{0:T(512)S(1)} %copy-done.2, bf16[1,32,32]{2,1,0:T(8,128)(2,1)S(1)} %copy-done.1), kind=kOutput, calls=%fused_computation.2 | convolution fusion | flops 70254592 | bytes 4206592 | tf_op jit(solution)/shard_map/ij,oajc->oaic/dot_general | solution.py:58
  (2 shorter events, 0.0 us)
Async XLA Ops:
  6.5 104.1 %copy-start = (bf16[3072,512]{1,0:T(8,128)(2,1)S(1)}, bf16[3072,512]{1,0:T(8,128)(2,1)}, u32[]{:S(2)}) copy-start(bf16[3072,512]{1,0:T(8,128)(2,1)} %param.9) | copy-start | bytes 9437188
  6.5 104.1 %all-gather.2.cloned.1.call-start = ((), (), s32[]{:S(2)}) async-start(), calls=%async_computation.2 | async-start | bytes 7077888 | tf_op jit(solution)/shard_map/all_gather | solution.py:36
  13.0 111.2 %all-to-all-start.1 = ((bf16[4,2,256]{2,1,0:T(2,128)(2,1)}), bf16[4,2,256]{2,1,0:T(2,128)(2,1)S(1)}, u32[]{:S(2)}, u32[]{:S(2)}) async-start(bf16[4,2,256]{2,1,0:T(2,128)(2,1)} %reshape.55), calls=%async_computation.1 | async-start | bytes 8192 | tf_op jit(solution)/shard_map/all_to_all | solution.py:51
  124.2 30.8 %copy-start.1 = (bf16[1,32,32]{2,1,0:T(8,128)(2,1)S(1)}, bf16[1,32,32]{2,1,0:T(8,128)(2,1)}, u32[]{:S(2)}) copy-start(bf16[1,32,32]{2,1,0:T(8,128)(2,1)} %param.15) | copy-start | bytes 6148
  124.2 30.8 %copy-start.2 = (f32[512]{0:T(512)S(1)}, f32[512]{0:T(512)}, u32[]{:S(2)}) copy-start(f32[512]{0:T(512)} %param.14) | copy-start | bytes 6148
  124.2 30.8 %all-to-all-start = ((bf16[4,16,32,512]{3,2,1,0:T(8,128)(2,1)}), bf16[4,16,32,512]{3,2,1,0:T(8,128)(2,1)}, u32[]{:S(2)}, u32[]{:S(2)}) async-start(bf16[4,16,32,512]{3,2,1,0:T(8,128)(2,1)} %bitcast.28), calls=%async_computation | async-start | bytes 4194304 | tf_op jit(solution)/shard_map/all_to_all | solution.py:44
Sparse Core Ops, SparseCore 0:
  9.8 100.7 all-gather.1
where the time goes:
time: 167 us; the launch traced here: 166 us
  waiting for transfers between devices  117 us (70%)
  matrix products  14 us (8%)
  between operations  13.4 us (8%)
  starting transfers between devices  10.2 us (6%)
  local copies, waits for them, and re-layouts  6.05 us (4%)
  other arithmetic  4.36 us (3%)
    all_gather x1, waiting for transfers between devices, shards(): lax.all_gather(masked.reshape(row_count, k_width), 'vir', axis=1, tiled=T...  92.7 us
    all_to_all x1, waiting for transfers between devices, shards(): lax.all_to_all(send_tiles.reshape(owner_count, capacity, tile_rows, col_c...  24.7 us
    dot_general x1, matrix products, shards(): jnp.dot(lax.all_gather(masked.reshape(row_count, k_width), 'vir', axis=1,...  7.17 us
    all_to_all x1, starting transfers between devices, shards(): lax.all_to_all(send_tiles.reshape(owner_count, capacity, tile_rows, col_c...  5.95 us
    all_to_all x1, starting transfers between devices, shards(): lax.all_to_all(send_energy.reshape(owner_count, capacity, tile_rows), 'oc...  4.25 us
    dot_general x1, matrix products, shards(): jnp.einsum('ij,oajc->oaic', weight, tiles_in, preferred_element_type=jnp....  3.66 us
  transfers between devices with their start and end apart: 3, of which 2 were waited for; matrix products, arithmetic and copies ran while one was open for 11% of the time, Pallas kernels for 0%

commit v1 on v0

v1 whole, which is shorter than its diff:
```python
import functools

import jax
import jax.numpy as jnp
from jax import lax
from jax.experimental import pallas as pl
from jax.experimental.pallas import tpu as pltpu
from jax.sharding import PartitionSpec as P

MESH = pl.DeviceIdType.MESH


def ladder_kernel(
    cfg, amps, ints, amp_mask, keep, own_s, own_v, occ, vir, mix, out,
    gath, ints_v, tiles, mix_all, own_all, own_tab, nxt,
    lsem, rsem_g, ssem_g, rsem_t, ssem_c, ssem_t, rsem_o, ssem_o,
):
    no, nv, td, tr, chunk_tiles, ahead, k_tile = cfg
    ng, nz = no // 2, nv // 2
    rows, kw = amps.shape
    cols = ints.shape[1]
    cr = chunk_tiles * tr
    nc = rows // cr
    cap = out.shape[0] // no
    o, v = lax.axis_index("occ"), lax.axis_index("vir")
    g, c = o // 2, o % 2
    z, y = v // 2, v % 2
    partner = {"occ": g * 2 + (1 - c), "vir": v}
    side = {"occ": o, "vir": z * 2 + (1 - y)}
    above = {"occ": o, "vir": (z + 1) * 2 + y}
    below = {"occ": o, "vir": (z - 1) * 2 + y}

    local = [
        pltpu.make_async_copy(own_v, own_all.at[o], lsem.at[0]),
        pltpu.make_async_copy(mix.at[0], mix_all.at[o], lsem.at[1]),
        pltpu.make_async_copy(amps, gath.at[v], lsem.at[2]),
        pltpu.make_async_copy(ints, ints_v, lsem.at[3]),
    ]
    for copy in local:
        copy.start()

    barrier = pltpu.get_barrier_semaphore()

    def greet(device):
        pl.semaphore_signal(barrier, inc=1, device_id=device, device_id_type=MESH)

    for d in range(1, no):
        greet({"occ": (o + d) % no, "vir": v})
    greet(side)

    @pl.when(z < nz - 1)
    def _():
        greet(above)

    @pl.when(z > 0)
    def _():
        greet(below)

    inner = jnp.where(z < nz - 1, 1, 0) + jnp.where(z > 0, 1, 0)
    pl.semaphore_wait(barrier, no + inner)

    def piece(src, slot, i, send_sem, device):
        window = pl.ds(pl.multiple_of(i * cr, cr), cr)
        return pltpu.make_async_remote_copy(
            src_ref=src.at[window], dst_ref=gath.at[slot, window], send_sem=send_sem,
            recv_sem=rsem_g.at[slot, i], device_id=device, device_id_type=MESH,
        )

    def spread(src, slot, i, up, down):
        zz = slot // 2
        if up:
            @pl.when(z < nz - 1)
            def _():
                piece(src, slot, i, ssem_g.at[0, zz], above).start()
        if down:
            @pl.when(z > 0)
            def _():
                piece(src, slot, i, ssem_g.at[1, zz], below).start()
        piece(src, slot, i, ssem_g.at[2, zz], side).start()

    def arrive(slot, i):
        piece(gath.at[slot], slot, i, ssem_g.at[2, 0], side).wait_recv()

    for i in range(min(ahead, nc)):
        spread(amps, v, i, True, True)

    def small(d, o2):
        peer = {"occ": (o + d) % no, "vir": v}
        return [
            pltpu.make_async_remote_copy(
                src_ref=own_v, dst_ref=own_all.at[o2], send_sem=ssem_o.at[0, d],
                recv_sem=rsem_o.at[0, o2], device_id=peer, device_id_type=MESH),
            pltpu.make_async_remote_copy(
                src_ref=mix.at[0], dst_ref=mix_all.at[o2], send_sem=ssem_o.at[1, d],
                recv_sem=rsem_o.at[1, o2], device_id=peer, device_id_type=MESH),
        ]

    for d in range(1, no):
        for copy in small(d, o):
            copy.start()
    for d in range(1, no):
        for copy in small(d, (o + d) % no):
            copy.wait_recv()
    for copy in local:
        copy.wait()
    table = pltpu.make_async_copy(own_all, own_tab, lsem.at[4])
    table.start()
    table.wait()

    def scan_source(s, carry):
        nxt[s, td] = td

        def back(n, following):
            t = td - 1 - n
            following = jnp.where(own_tab[s, 0, t] == o, t, following)
            nxt[s, t] = following
            return following

        lax.fori_loop(0, td, back, jnp.int32(td))
        return carry

    lax.fori_loop(0, no, scan_source, 0)

    def tile_piece(o2, i, send_sem, device):
        window = pl.ds(i * chunk_tiles, chunk_tiles)
        return pltpu.make_async_remote_copy(
            src_ref=tiles.at[o2, window], dst_ref=tiles.at[o2, window], send_sem=send_sem,
            recv_sem=rsem_t.at[o2, i], device_id=device, device_id_type=MESH,
        )

    def group_of(d):
        return ((g + d) % ng) * 2

    def hand_on(i):
        for d in range(1, ng):
            o2 = group_of(d) + c
            tile_piece(o2, i, ssem_c.at[d], partner).wait_recv()
            tile_piece(o2, i, ssem_c.at[d], partner).start()

    def compute(i):
        first = pl.multiple_of(i * cr, cr)
        total = jnp.zeros((cr, cols), jnp.float32)
        for slot in range(nv):
            block = gath[slot, pl.ds(first, cr), :]
            column = slot * kw + lax.broadcasted_iota(jnp.int32, (1, kw), 1)
            low, high = slot * kw // k_tile, ((slot + 1) * kw - 1) // k_tile
            parts = []
            for n in range(chunk_tiles):
                t = i * chunk_tiles + n
                flag = jnp.full((1, kw), amp_mask[low, t].astype(jnp.float32))
                for s in range(low + 1, high + 1):
                    flag = jnp.where(column >= s * k_tile, amp_mask[s, t].astype(jnp.float32), flag)
                flag = jnp.broadcast_to(flag, (tr, kw)).astype(jnp.bfloat16)
                parts.append(block[n * tr:(n + 1) * tr] * flag)
            total += jnp.dot(
                jnp.concatenate(parts, axis=0), ints_v[slot * kw:(slot + 1) * kw, :],
                preferred_element_type=jnp.float32,
            )
        ladder = total.astype(jnp.bfloat16)
        occ_col = jnp.transpose(jnp.broadcast_to(occ[i], (128, cr)))[:, :1]
        for n in range(chunk_tiles):
            t = i * chunk_tiles + n
            kept = ladder[n * tr:(n + 1) * tr] * keep[0, t].astype(jnp.float32).astype(jnp.bfloat16)
            mixed = jnp.dot(mix_all[own_s[0, t]], kept, preferred_element_type=jnp.float32)
            denominator = vir[...] - occ_col[n * tr:(n + 1) * tr]
            tiles[o, t] = (mixed / denominator).astype(jnp.bfloat16)

    def step(i, carry):
        @pl.when(i + ahead < nc)
        def _():
            spread(amps, v, i + ahead, True, True)

        for j in range(1, nz):
            @pl.when(z >= j)
            def _():
                slot = (z - j) * 2 + y
                arrive(slot, i)
                spread(gath.at[slot], slot, i, True, False)

            @pl.when(z + j < nz)
            def _():
                slot = (z + j) * 2 + y
                arrive(slot, i)
                spread(gath.at[slot], slot, i, False, True)

        for zz in range(nz):
            arrive(zz * 2 + (1 - y), i)
        compute(i)
        for d in range(1, ng):
            tile_piece(o, i, ssem_t.at[d], {"occ": group_of(d) + c, "vir": v}).start()
        tile_piece(o, i, ssem_c.at[0], partner).start()

        @pl.when(i > 0)
        def _():
            hand_on(i - 1)

        return carry

    lax.fori_loop(0, nc, step, 0)
    hand_on(nc - 1)

    def last(i, carry):
        for d in range(ng):
            tile_piece(group_of(d) + (1 - c), i, ssem_c.at[d], partner).wait_recv()
        return carry

    lax.fori_loop(0, nc, last, 0)

    def source(s, carry):
        def slot(k, position):
            t = nxt[s, position]
            tile = tiles[s, jnp.minimum(t, td - 1)]
            out[s * cap + k] = jnp.where(t < td, tile, jnp.zeros_like(tile))
            return jnp.minimum(t + 1, td)

        lax.fori_loop(0, cap, slot, jnp.int32(0))
        return carry

    lax.fori_loop(0, no, source, 0)

    def sent(whole, send_sem, recv_sem, device):
        pltpu.make_async_remote_copy(
            src_ref=whole, dst_ref=whole, send_sem=send_sem, recv_sem=recv_sem,
            device_id=device, device_id_type=MESH).wait_send()

    for zz in range(nz):
        @pl.when((z < nz - 1) & (zz <= z))
        def _():
            sent(gath.at[zz], ssem_g.at[0, zz], rsem_g.at[0, 0], side)

        @pl.when((z > 0) & (zz >= z))
        def _():
            sent(gath.at[zz], ssem_g.at[1, zz], rsem_g.at[0, 0], side)

        sent(gath.at[zz], ssem_g.at[2, zz], rsem_g.at[0, 0], side)
    for d in range(ng):
        sent(tiles.at[d], ssem_c.at[d], rsem_t.at[0, 0], partner)
        if d:
            sent(tiles.at[d], ssem_t.at[d], rsem_t.at[0, 0], partner)
    for d in range(1, no):
        for copy in small(d, o):
            copy.wait_send()


def shards(no, nv, amps, ints, amp_mask, keep_mask, owners, occ_energy, vir_energy, mix):
    td, k_tiles = amp_mask.shape
    rows, kw = amps.shape
    tr = rows // td
    cols = ints.shape[1]
    k_tile = ints.shape[0] // k_tiles
    cap = max(2, 2 * td // no)
    chunk_tiles = max(1, min(td, 128 // tr))
    nc = td // chunk_tiles
    cfg = (no, nv, td, tr, chunk_tiles, 2, k_tile)
    smem = pl.BlockSpec(memory_space=pltpu.SMEM)
    vmem = pl.BlockSpec(memory_space=pltpu.VMEM)
    hbm = pl.BlockSpec(memory_space=pl.ANY)
    ng, nz = no // 2, nv // 2
    own = owners.reshape(1, td)
    return pl.pallas_call(
        functools.partial(ladder_kernel, cfg),
        out_shape=jax.ShapeDtypeStruct((no * cap, tr, cols), jnp.bfloat16),
        in_specs=[hbm, hbm, smem, smem, smem, vmem, vmem, vmem, vmem],
        out_specs=vmem,
        scratch_shapes=[
            pltpu.VMEM((nv, rows, kw), jnp.bfloat16),
            pltpu.VMEM(ints.shape, jnp.bfloat16),
            pltpu.VMEM((no, td, tr, cols), jnp.bfloat16),
            pltpu.VMEM((no, tr, tr), jnp.bfloat16),
            pltpu.VMEM((no, 1, td), jnp.int32),
            pltpu.SMEM((no, 1, td), jnp.int32),
            pltpu.SMEM((no, td + 1), jnp.int32),
            pltpu.SemaphoreType.DMA((5,)),
            pltpu.SemaphoreType.DMA((nv, nc)),
            pltpu.SemaphoreType.DMA((3, nz)),
            pltpu.SemaphoreType.DMA((no, nc)),
            pltpu.SemaphoreType.DMA((ng,)),
            pltpu.SemaphoreType.DMA((ng,)),
            pltpu.SemaphoreType.DMA((2, no)),
            pltpu.SemaphoreType.DMA((2, no)),
        ],
        compiler_params=pltpu.CompilerParams(
            collective_id=0, has_side_effects=True, vmem_limit_bytes=60 * 1024 * 1024
        ),
    )(
        amps, ints, amp_mask.T, keep_mask.reshape(1, td), own, own,
        occ_energy.astype(jnp.float32).reshape(nc, 1, chunk_tiles * tr),
        vir_energy.reshape(1, cols), mix,
    )


def solution(mesh):
    in_specs = (
        P("occ", "vir"),
        P(None, "vir"),
        P("occ", None),
        P("occ", "vir"),
        P("occ", None),
        P("occ"),
        P("vir"),
        P("occ", None, None),
    )
    body = functools.partial(shards, mesh.shape["occ"], mesh.shape["vir"])
    return jax.shard_map(
        body, mesh=mesh, in_specs=in_specs, out_specs=P("occ", None, "vir"), check_vma=False
    )
```

time: 167 us -> 105 us (0.63)
  waiting for transfers between devices: 117 us -> 0 us
  Pallas kernels: 0 us -> 100 us
  matrix products: 14 us -> 0 us
  between operations: 13.4 us -> 0.01 us
  starting transfers between devices: 10.2 us -> 0 us
  other arithmetic: 4.36 us -> 1.27 us
  local copies, waits for them, and re-layouts: 6.05 us -> 3.16 us
    pallas_call x0 -> x1, Pallas kernels: none -> 100 us  [shards(): pl.pallas_call(functools.partial(ladder_kernel, cfg), out_shape=jax.Shape...]
    all_gather x1 -> x0, waiting for transfers between devices: 92.7 us -> none  [shards(): lax.all_gather(masked.reshape(row_count, k_width), 'vir', axis=1, tiled=T...]
    all_to_all x2 -> x0, waiting for transfers between devices: 24.7 us -> none  [the longest x1 24.7 us: shards(): lax.all_to_all(send_tiles.reshape(owner_count, capacity, tile_rows, col_c...]
    dot_general x5 -> x0, matrix products: 14 us -> none  [the longest x1 7.17 us: shards(): jnp.dot(lax.all_gather(masked.reshape(row_count, k_width), 'vir', axis=1,...]
    all_to_all x2 -> x0, starting transfers between devices: 10.2 us -> none  [the longest x1 5.95 us: shards(): lax.all_to_all(send_tiles.reshape(owner_count, capacity, tile_rows, col_c...]
    reshape x2 -> x0, local copies, waits for them, and re-layouts: 3.09 us -> none  [the longest x1 2.33 us: shards(): ladder.astype(jnp.bfloat16).reshape(tiles_dev, tile_rows * col_count)]
    mul x2 -> x0, other arithmetic: 2.77 us -> none  [the longest x1 2.11 us: shards(): masked = amps.reshape(tiles_dev, tile_rows, k_width) * col_mask[:, None, :]]
  transfers between devices with their start and end apart: 3 -> 0, of which waited for: 2 -> 0; matrix products, arithmetic and copies ran while one was open for 11% -> 0% of each run, Pallas kernels for 0% -> 0%
where the time goes in v1:
time: 105 us
  Pallas kernels  100 us (95%)
  local copies, waits for them, and re-layouts  3.16 us (3%)
  other arithmetic  1.27 us (1%)
    pallas_call x1, Pallas kernels, shards(): pl.pallas_call(functools.partial(ladder_kernel, cfg), out_shape=jax.Shape...  100 us
    unnamed x1, local copies, waits for them, and re-layouts  3.16 us

profile of v1, /device:TPU:1, one launch (start us, length us, event | category | flops | bytes accessed | tf_op | source)
XLA Modules:
  0.0 104.9 jit_solution(7257804396923496639)
XLA Ops:
  0.0 1.3 %reshape.19 = f32[1024]{0:T(1024)} convert(bf16[1024]{0:T(1024)(128)(2,1)} %param.13) | non-fusion elementwise | flops 1024 | bytes 6144 | tf_op jit(solution)/shard_map/reshape | solution.py:287
  1.3 100.5 %shard_map.82 = bf16[64,32,512]{2,1,0:T(8,128)(2,1)} custom-call(bf16[1024,384]{1,0:T(8,128)(2,1)} %amps.1, bf16[3072,512]{1,0:T(8,128)(2,1)} %ints.1, s32[6,32]{1,0:T(8,128)} %bitcast.6, s32[1,32]{1,0:T(1,128)} %bitcast.10, s32[1,32]{1,0:T(1,128)} %bitcast.8, s32[1,32]{1,0:T(1,128)} %bitcast.9, f32[8,1,128]{2,1,0:T(1,128)} %bitcast.5, f32[1,512]{1,0:T(1,128)} %bitcast.7, ...), custom_call_target="tpu_custom_call" | custom-call | tf_op jit(solution)/shard_map/pallas_call | solution.py:260
  101.8 3.2 %copy.10 = bf16[64,32,512]{2,1,0:T(8,128)(2,1)} copy(bf16[64,32,512]{2,1,0:T(8,128)(2,1)} %shard_map.82) | data formatting | bytes 4194304

commit v2 on v1

--- a/solution.py
+++ b/solution.py
@@ -12,10 +12,10 @@
 
 def ladder_kernel(
     cfg, amps, ints, amp_mask, keep, own_s, own_v, occ, vir, mix, out,
-    gath, ints_v, tiles, mix_all, own_all, own_tab, nxt,
+    gath, ints_v, occ_col, tiles, mix_all, own_all, own_tab, nxt,
     lsem, rsem_g, ssem_g, rsem_t, ssem_c, ssem_t, rsem_o, ssem_o,
 ):
-    no, nv, td, tr, chunk_tiles, ahead, k_tile = cfg
+    no, nv, td, tr, chunk_tiles, k_tile, ahead, ahead_side, stagger, lag, side_every = cfg
     ng, nz = no // 2, nv // 2
     rows, kw = amps.shape
     cols = ints.shape[1]
@@ -32,9 +32,8 @@
 
     local = [
         pltpu.make_async_copy(own_v, own_all.at[o], lsem.at[0]),
+        pltpu.make_async_copy(ints, ints_v, lsem.at[3]),
         pltpu.make_async_copy(mix.at[0], mix_all.at[o], lsem.at[1]),
-        pltpu.make_async_copy(amps, gath.at[v], lsem.at[2]),
-        pltpu.make_async_copy(ints, ints_v, lsem.at[3]),
     ]
     for copy in local:
         copy.start()
@@ -66,23 +65,28 @@
             recv_sem=rsem_g.at[slot, i], device_id=device, device_id_type=MESH,
         )
 
-    def spread(src, slot, i, up, down):
-        zz = slot // 2
+    def side_first(i):
+        return i % side_every == side_every // 2
+
+    def spread(src, slot, i, up, down, across):
         if up:
             @pl.when(z < nz - 1)
             def _():
-                piece(src, slot, i, ssem_g.at[0, zz], above).start()
+                piece(src, slot, i, ssem_g.at[0, slot], above).start()
         if down:
             @pl.when(z > 0)
             def _():
-                piece(src, slot, i, ssem_g.at[1, zz], below).start()
-        piece(src, slot, i, ssem_g.at[2, zz], side).start()
+                piece(src, slot, i, ssem_g.at[1, slot], below).start()
+        if across:
+            piece(src, slot, i, ssem_g.at[2, slot], side).start()
 
     def arrive(slot, i):
         piece(gath.at[slot], slot, i, ssem_g.at[2, 0], side).wait_recv()
 
-    for i in range(min(ahead, nc)):
-        spread(amps, v, i, True, True)
+    for i in range(min(ahead_side, nc)):
+        if i < ahead:
+            spread(amps, v, i, True, True, False)
+        spread(amps, v, i, False, False, True)
 
     def small(d, o2):
         peer = {"occ": (o + d) % no, "vir": v}
@@ -98,28 +102,36 @@
     for d in range(1, no):
         for copy in small(d, o):
             copy.start()
-    for d in range(1, no):
-        for copy in small(d, (o + d) % no):
-            copy.wait_recv()
-    for copy in local:
-        copy.wait()
-    table = pltpu.make_async_copy(own_all, own_tab, lsem.at[4])
-    table.start()
-    table.wait()
-
-    def scan_source(s, carry):
-        nxt[s, td] = td
-
-        def back(n, following):
-            t = td - 1 - n
-            following = jnp.where(own_tab[s, 0, t] == o, t, following)
-            nxt[s, t] = following
-            return following
-
-        lax.fori_loop(0, td, back, jnp.int32(td))
-        return carry
-
-    lax.fori_loop(0, no, scan_source, 0)
+
+    def prepare():
+        for d in range(1, no):
+            for copy in small(d, (o + d) % no):
+                copy.wait_recv()
+        for copy in local:
+            copy.wait()
+        table = pltpu.make_async_copy(own_all, own_tab, lsem.at[2])
+        table.start()
+        table.wait()
+
+        def scan_source(s, carry):
+            nxt[s, td] = td
+
+            def back(n, following):
+                t = td - 1 - n
+                following = jnp.where(own_tab[s, 0, t] == o, t, following)
+                nxt[s, t] = following
+                return following
+
+            lax.fori_loop(0, td, back, jnp.int32(td))
+            return carry
+
+        lax.fori_loop(0, no, scan_source, 0)
+
+    gath[v] = amps[...]
+    lanes = occ.shape[1]
+    for r in range(occ.shape[0]):
+        row = jnp.broadcast_to(occ[...].astype(jnp.float32)[r:r + 1], (128, lanes))
+        occ_col[r * lanes:(r + 1) * lanes, :] = jnp.transpose(row)
 
     def tile_piece(o2, i, send_sem, device):
         window = pl.ds(i * chunk_tiles, chunk_tiles)
@@ -157,47 +169,78 @@
                 preferred_element_type=jnp.float32,
             )
         ladder = total.astype(jnp.bfloat16)
-        occ_col = jnp.transpose(jnp.broadcast_to(occ[i], (128, cr)))[:, :1]
         for n in range(chunk_tiles):
             t = i * chunk_tiles + n
             kept = ladder[n * tr:(n + 1) * tr] * keep[0, t].astype(jnp.float32).astype(jnp.bfloat16)
             mixed = jnp.dot(mix_all[own_s[0, t]], kept, preferred_element_type=jnp.float32)
-            denominator = vir[...] - occ_col[n * tr:(n + 1) * tr]
+            energy = occ_col[pl.ds(pl.multiple_of(t * tr, tr), tr), :]
+            denominator = vir[...] - jnp.concatenate([energy] * (cols // 128), axis=1)
             tiles[o, t] = (mixed / denominator).astype(jnp.bfloat16)
 
-    def step(i, carry):
-        @pl.when(i + ahead < nc)
-        def _():
-            spread(amps, v, i + ahead, True, True)
-
-        for j in range(1, nz):
-            @pl.when(z >= j)
+    def within(i, body):
+        @pl.when((i >= 0) & (i < nc))
+        def _():
+            body(i)
+
+    def send_own(i):
+        spread(amps, v, i, True, True, False)
+
+    def send_side(i):
+        spread(amps, v, i, False, False, True)
+
+    def turn(i):
+        @pl.when(side_first(i))
+        def _():
+            slot = z * 2 + (1 - y)
+            arrive(slot, i)
+            spread(gath.at[slot], slot, i, True, True, False)
+
+    def forward(j, i):
+        for step_z, up in ((-j, True), (j, False)):
+            near = z + step_z
+
+            @pl.when((near >= 0) & (near < nz))
             def _():
-                slot = (z - j) * 2 + y
+                slot = near * 2 + y
+                other = near * 2 + (1 - y)
                 arrive(slot, i)
-                spread(gath.at[slot], slot, i, True, False)
-
-            @pl.when(z + j < nz)
-            def _():
-                slot = (z + j) * 2 + y
-                arrive(slot, i)
-                spread(gath.at[slot], slot, i, False, True)
-
-        for zz in range(nz):
-            arrive(zz * 2 + (1 - y), i)
+                spread(gath.at[slot], slot, i, up, not up, False)
+
+                @pl.when(side_first(i))
+                def _():
+                    arrive(other, i)
+                    spread(gath.at[other], other, i, up, not up, False)
+
+                @pl.when(jnp.logical_not(side_first(i)))
+                def _():
+                    spread(gath.at[slot], slot, i, False, False, True)
+
+    def finish(i):
+        @pl.when(i == 0)
+        def _():
+            prepare()
+
+        @pl.when(jnp.logical_not(side_first(i)))
+        def _():
+            for zz in range(nz):
+                arrive(zz * 2 + (1 - y), i)
+
         compute(i)
         for d in range(1, ng):
             tile_piece(o, i, ssem_t.at[d], {"occ": group_of(d) + c, "vir": v}).start()
         tile_piece(o, i, ssem_c.at[0], partner).start()
 
-        @pl.when(i > 0)
-        def _():
-            hand_on(i - 1)
-
+    def step(s, carry):
+        within(s + ahead, send_own)
+        within(s + ahead_side, send_side)
+        within(s, turn)
+        for j in range(1, nz):
+            within(s - stagger * j, functools.partial(forward, j))
+        within(s - lag, finish)
+        within(s - lag - 1, hand_on)
         return carry
 
-    lax.fori_loop(0, nc, step, 0)
-    hand_on(nc - 1)
+    lax.fori_loop(0, nc + lag + 1, step, 0)
 
     def last(i, carry):
         for d in range(ng):
@@ -223,16 +266,30 @@
             src_ref=whole, dst_ref=whole, send_sem=send_sem, recv_sem=recv_sem,
             device_id=device, device_id_type=MESH).wait_send()
 
+    turned = sum(1 for i in range(nc) if side_first(i)) * cr
+    full = gath.shape[1]
     for zz in range(nz):
-        @pl.when((z < nz - 1) & (zz <= z))
-        def _():
-            sent(gath.at[zz], ssem_g.at[0, zz], rsem_g.at[0, 0], side)
-
-        @pl.when((z > 0) & (zz >= z))
-        def _():
-            sent(gath.at[zz], ssem_g.at[1, zz], rsem_g.at[0, 0], side)
-
-        sent(gath.at[zz], ssem_g.at[2, zz], rsem_g.at[0, 0], side)
+        for slot, count in ((zz * 2 + y, full), (zz * 2 + (1 - y), turned)):
+            if count:
+                whole = gath.at[zz, pl.ds(0, count)]
+
+                @pl.when((z < nz - 1) & (zz <= z))
+                def _():
+                    sent(whole, ssem_g.at[0, slot], rsem_g.at[0, 0], side)
+
+                @pl.when((z > 0) & (zz >= z))
+                def _():
+                    sent(whole, ssem_g.at[1, slot], rsem_g.at[0, 0], side)
+
+        @pl.when(zz == z)
+        def _():
+            sent(gath.at[zz], ssem_g.at[2, v], rsem_g.at[0, 0], side)
+
+        if full > turned:
+            @pl.when(zz != z)
+            def _():
+                part = gath.at[zz, pl.ds(0, full - turned)]
+                sent(part, ssem_g.at[2, zz * 2 + y], rsem_g.at[0, 0], side)
     for d in range(ng):
         sent(tiles.at[d], ssem_c.at[d], rsem_t.at[0, 0], partner)
         if d:
@@ -251,28 +308,30 @@
     cap = max(2, 2 * td // no)
     chunk_tiles = max(1, min(td, 128 // tr))
     nc = td // chunk_tiles
-    cfg = (no, nv, td, tr, chunk_tiles, 2, k_tile)
+    ahead, ahead_side, stagger, side_every = 2, 6, 1, 8
+    lag = stagger * (nv // 2 - 1) + 1
+    cfg = (no, nv, td, tr, chunk_tiles, k_tile, ahead, ahead_side, stagger, lag, side_every)
     smem = pl.BlockSpec(memory_space=pltpu.SMEM)
     vmem = pl.BlockSpec(memory_space=pltpu.VMEM)
-    hbm = pl.BlockSpec(memory_space=pl.ANY)
     ng, nz = no // 2, nv // 2
     own = owners.reshape(1, td)
     return pl.pallas_call(
         functools.partial(ladder_kernel, cfg),
         out_shape=jax.ShapeDtypeStruct((no * cap, tr, cols), jnp.bfloat16),
-        in_specs=[hbm, hbm, smem, smem, smem, vmem, vmem, vmem, vmem],
+        in_specs=[vmem, pl.BlockSpec(memory_space=pl.ANY), smem, smem, smem, vmem, vmem, vmem, vmem],
         out_specs=vmem,
         scratch_shapes=[
             pltpu.VMEM((nv, rows, kw), jnp.bfloat16),
             pltpu.VMEM(ints.shape, jnp.bfloat16),
+            pltpu.VMEM((rows, 128), jnp.float32),
             pltpu.VMEM((no, td, tr, cols), jnp.bfloat16),
             pltpu.VMEM((no, tr, tr), jnp.bfloat16),
             pltpu.VMEM((no, 1, td), jnp.int32),
             pltpu.SMEM((no, 1, td), jnp.int32),
             pltpu.SMEM((no, td + 1), jnp.int32),
-            pltpu.SemaphoreType.DMA((5,)),
+            pltpu.SemaphoreType.DMA((4,)),
             pltpu.SemaphoreType.DMA((nv, nc)),
-            pltpu.SemaphoreType.DMA((3, nz)),
+            pltpu.SemaphoreType.DMA((3, nv)),
             pltpu.SemaphoreType.DMA((no, nc)),
             pltpu.SemaphoreType.DMA((ng,)),
             pltpu.SemaphoreType.DMA((ng,)),
@@ -284,7 +343,7 @@
         ),
     )(
         amps, ints, amp_mask.T, keep_mask.reshape(1, td), own, own,
-        occ_energy.astype(jnp.float32).reshape(nc, 1, chunk_tiles * tr),
+        occ_energy.reshape(rows // 128, 128),
         vir_energy.reshape(1, cols), mix,
     )
 

time: 105 us -> 82.4 us (0.78)
  Pallas kernels: 100 us -> 79.1 us
  other arithmetic: 1.27 us -> 0 us
    pallas_call x1, Pallas kernels: 100 us -> 79.1 us  [shards(): pl.pallas_call(functools.partial(ladder_kernel, cfg), out_shape=jax.Shape...]
    reshape x1 -> x0, other arithmetic: 1.27 us -> none  [shards(): occ_energy.astype(jnp.float32).reshape(nc, 1, chunk_tiles * tr)]
where the time goes in v2:
time: 82.4 us; the launch traced here: 82.3 us
  Pallas kernels  79.1 us (96%)
  local copies, waits for them, and re-layouts  3.16 us (4%)
    pallas_call x1, Pallas kernels, shards(): pl.pallas_call(functools.partial(ladder_kernel, cfg), out_shape=jax.Shape...  79.1 us
    unnamed x1, local copies, waits for them, and re-layouts  3.16 us

profile of v2, /device:TPU:1, one launch (start us, length us, event | category | flops | bytes accessed | tf_op | source)
XLA Modules:
  0.0 82.3 jit_solution(16683141356703357548)
XLA Ops:
  0.0 79.1 %shard_map.82 = bf16[64,32,512]{2,1,0:T(8,128)(2,1)} custom-call(bf16[1024,384]{1,0:T(8,128)(2,1)} %amps.1, bf16[3072,512]{1,0:T(8,128)(2,1)} %ints.1, s32[6,32]{1,0:T(8,128)} %bitcast.5, s32[1,32]{1,0:T(1,128)} %bitcast.10, s32[1,32]{1,0:T(1,128)} %bitcast.8, s32[1,32]{1,0:T(1,128)} %bitcast.9, bf16[8,128]{1,0:T(8,128)(2,1)} %bitcast.6, f32[1,512]{1,0:T(1,128)} %bitcast.7, ...), custom_call_target="tpu_custom_call" | custom-call | tf_op jit(solution)/shard_map/pallas_call | solution.py:318
  79.1 3.2 %copy.10 = bf16[64,32,512]{2,1,0:T(8,128)(2,1)} copy(bf16[64,32,512]{2,1,0:T(8,128)(2,1)} %shard_map.82) | data formatting | bytes 4194304
